TPU v7x, 32 devices: a whole 2x2x4 slice. The times are simulated.
32 devices in a mesh: seq: 8 (over z, y), feat: 4 (over x, core).
Axes of the slice: x: 2, y: 2, z: 4, core: 2. Of those that a mesh axis runs over, the one named last changes fastest.
Arguments:
- activations_in: bfloat16 [6144, 512], P('seq', 'feat'), may hold values from -6 to 6
- cotangent: bfloat16 [6144, 512], P('seq', 'feat'), may hold values from -6 to 6
- seq_start: int32 [16], P('seq'), may hold values from 0 to 768, as said below
- seq_length: int32 [16], P('seq'), may hold values from 0 to 768, as said below
- input_matrix: float32 [2, 512, 768], P(None, 'feat'), may hold values from -0.25 to 0.25
- output_matrix: float32 [2, 1536, 512], P(None, None, 'feat'), may hold values from -1.25 to 1.25
- gate_matrix: float32 [2, 512, 512], P(None, None, 'feat'), may hold values from -0.25 to 0.25
- feature_vectors: float32 [2, 4, 512], P(None, None, 'feat'), may hold values from 0.1 to 1.9
- state_vectors: float32 [2, 3, 384], replicated, may hold values from -20 to 20, as said below
- velocity_input: float32 [2, 512, 768], P(None, 'feat'), may hold values from -6 to 6
- velocity_output: float32 [2, 1536, 512], P(None, None, 'feat'), may hold values from -6 to 6
- velocity_gate: float32 [2, 512, 512], P(None, None, 'feat'), may hold values from -6 to 6
- velocity_feature: float32 [2, 4, 512], P(None, None, 'feat'), may hold values from -6 to 6
- velocity_state: float32 [2, 3, 384], replicated, may hold values from -6 to 6
- average_input: float32 [2, 512, 768], P(None, 'feat'), may hold values from -0.25 to 0.25
- average_output: float32 [2, 1536, 512], P(None, None, 'feat'), may hold values from -1.25 to 1.25
- average_gate: float32 [2, 512, 512], P(None, None, 'feat'), may hold values from -0.25 to 0.25
- average_feature: float32 [2, 4, 512], P(None, None, 'feat'), may hold values from 0.1 to 1.9
- average_state: float32 [2, 3, 384], replicated, may hold values from -3 to 1
Outputs:
- activations_out: float32 [6144, 512], P('seq', 'feat')
- input_gradient: float32 [6144, 512], P('seq', 'feat')
- gradient_input: float32 [2, 512, 768], P(None, 'feat')
- gradient_output: float32 [2, 1536, 512], P(None, None, 'feat')
- gradient_gate: float32 [2, 512, 512], P(None, None, 'feat')
- gradient_feature: float32 [2, 4, 512], P(None, None, 'feat')
- gradient_state: float32 [2, 3, 384], replicated
- updated_input: float32 [2, 512, 768], P(None, 'feat')
- updated_output: float32 [2, 1536, 512], P(None, None, 'feat')
- updated_gate: float32 [2, 512, 512], P(None, None, 'feat')
- updated_feature: float32 [2, 4, 512], P(None, None, 'feat')
- state_change: float32 [2, 3, 384], replicated
- momentum_input: float32 [2, 512, 768], P(None, 'feat')
- momentum_output: float32 [2, 1536, 512], P(None, None, 'feat')
- momentum_gate: float32 [2, 512, 512], P(None, None, 'feat')
- momentum_feature: float32 [2, 4, 512], P(None, None, 'feat')
- momentum_state: float32 [2, 3, 384], replicated
- smoothed_input: float32 [2, 512, 768], P(None, 'feat')
- smoothed_output: float32 [2, 1536, 512], P(None, None, 'feat')
- smoothed_gate: float32 [2, 512, 512], P(None, None, 'feat')
- smoothed_feature: float32 [2, 4, 512], P(None, None, 'feat')
- smoothed_state: float32 [2, 3, 384], replicated
Inputs may be any that keep to these rules, and one draw needn't show every extreme that they name: `seq_length`: sequences of a device lie in its own buffer, ordered and without intersection; one device holds a single sequence of 768 tokens and an empty slot, every other device two sequences of 192 to 384 tokens. `seq_start`: positions within a device's buffer; a slot of length zero starts at 768. `state_vectors`: rows hold log(-Re Lambda), Im Lambda and the log timestep.
All inputs are finite; a program needn't handle non-finite values.
Results may differ from a plain program's by a relative error of at most 0.012.
The roundings to bfloat16 on the way count: a program that leaves them out, or rounds other values in their place, can miss the bound.
Values may be sent and summed in bfloat16 or wider, within the bound.
A program may use at most 448 MiB of HBM per device.

v0:
```python
import math
import jax
import jax.numpy as jnp
from jax import lax
from jax.sharding import PartitionSpec as P

epsilon = 1e-05
momentum = 0.9
smoothing = 0.5
slow_rate = 0.02
main_rate = 0.05
weight_decay = 0.1


def smooth(value):
    return jax.nn.gelu(value, approximate=False)


def combine(earlier, later):
    mult_real = later[0] * earlier[0] - later[1] * earlier[1]
    mult_imag = later[0] * earlier[1] + later[1] * earlier[0]
    add_real = later[0] * earlier[2] - later[1] * earlier[3] + later[2]
    add_imag = later[0] * earlier[3] + later[1] * earlier[2] + later[3]
    return (mult_real, mult_imag, add_real, add_imag)


def masks_of(starts, lengths, count):
    position = jnp.arange(count, dtype=jnp.int32)[:, None]
    begin = starts[None, :]
    finish = begin + lengths[None, :]
    inside = (position >= begin) & (position < finish)
    alive = jnp.any(inside, 1)
    opening = jnp.any(inside & (position == begin), 1)
    closing = jnp.any(inside & (position == finish - 1), 1)
    return (
        alive.astype(jnp.float32),
        (alive & ~opening).astype(jnp.float32),
        (alive & ~closing).astype(jnp.float32),
    )


def prefix(current, backward):
    length = current[2].shape[0]
    offset = 1
    while offset < length:

        def shifted(value):
            filler = jnp.zeros((offset,) + value.shape[1:], value.dtype)
            if backward:
                return jnp.concatenate([value[offset:], filler], 0)
            return jnp.concatenate([filler, value[: length - offset]], 0)

        earlier = tuple((shifted(value) for value in current))
        current = combine(earlier, current)
        offset = offset * 2
    return current


def scan_states(drive, state_row, alive, carry_prev, carry_next):
    width = state_row.shape[1]
    rate = -jnp.exp(state_row[0])
    frequency = state_row[1]
    timestep = jnp.exp(state_row[2])
    decay = jnp.exp(rate * timestep)
    angle = frequency * timestep
    pole_real = decay * jnp.cos(angle)
    pole_imag = decay * jnp.sin(angle)
    denom = rate * rate + frequency * frequency
    factor_real = ((pole_real - 1.0) * rate + pole_imag * frequency) / denom
    factor_imag = (pole_imag * rate - (pole_real - 1.0) * frequency) / denom
    drive_real = drive[:, :width]
    drive_imag = drive[:, width:]
    input_real = (drive_real * factor_real - drive_imag * factor_imag) * alive[:, None]
    input_imag = (drive_real * factor_imag + drive_imag * factor_real) * alive[:, None]
    ahead = prefix(
        (carry_prev[:, None] * pole_real, carry_prev[:, None] * pole_imag, input_real, input_imag),
        False,
    )
    behind = prefix(
        (carry_next[:, None] * pole_real, carry_next[:, None] * pole_imag, input_real, input_imag),
        True,
    )
    return jnp.concatenate([ahead[2], ahead[3], behind[2], behind[3]], 1)


def update(weight, gradient, velocity, average, rate, decay):
    adjusted = gradient + decay * weight
    velocity_new = momentum * velocity + adjusted
    change = -rate * (adjusted + momentum * velocity_new)
    weight_new = weight + change
    average_new = smoothing * average + (1.0 - smoothing) * weight_new
    return (weight_new, velocity_new, average_new, change)


def contract_rows(left, right):
    return lax.dot_general(
        left, right, (((0,), (0,)), ((), ())), preferred_element_type=jnp.float32
    )


def contract_cols(left, right):
    return lax.dot_general(
        left, right, (((1,), (1,)), ((), ())), preferred_element_type=jnp.float32
    )


def moments(stream):
    whole = lax.all_gather(stream, "feat", axis=1, tiled=True)
    center = jnp.mean(whole, 1, keepdims=True)
    spread = whole - center
    variance = jnp.mean(spread * spread, 1, keepdims=True)
    return (center, lax.rsqrt(variance + epsilon))


def back_moments(unit_grad, unit):
    spread_grad, crossed = (
        lax.all_gather(unit_grad, "feat", axis=1, tiled=True),
        lax.all_gather(unit_grad * unit, "feat", axis=1, tiled=True),
    )
    return (jnp.mean(spread_grad, 1, keepdims=True), jnp.mean(crossed, 1, keepdims=True))


def state_forward(normed_low, in_low, state_row, masks):
    partial_drive = jnp.dot(normed_low, in_low, preferred_element_type=jnp.float32)
    drive = lax.psum(partial_drive, "feat")
    states = scan_states(drive, state_row, masks[0], masks[1], masks[2])
    return (drive, states.astype(jnp.bfloat16))


def state_backward(drive, state_row, masks, mixed_low, out_low):

    def scanned(drive_in, rows_in):
        return scan_states(drive_in, rows_in, masks[0], masks[1], masks[2])

    partial_states = contract_cols(mixed_low, out_low)
    states_grad = lax.psum(partial_states, "feat")
    unused, pull = jax.vjp(scanned, drive, state_row)
    drive_grad, row_grad = pull(states_grad)
    return (drive_grad.astype(jnp.bfloat16), row_grad)


def body(
    activations_in,
    cotangent,
    seq_start,
    seq_length,
    input_matrix,
    output_matrix,
    gate_matrix,
    feature_vectors,
    state_vectors,
    velocity_input,
    velocity_output,
    velocity_gate,
    velocity_feature,
    velocity_state,
    average_input,
    average_output,
    average_gate,
    average_feature,
    average_state,
):
    count = activations_in.shape[0]
    layers = input_matrix.shape[0]
    masks = masks_of(seq_start, seq_length, count)
    stream = activations_in.astype(jnp.float32)
    saved = []
    for layer in range(layers):
        in_low = input_matrix[layer].astype(jnp.bfloat16)
        out_low = output_matrix[layer].astype(jnp.bfloat16)
        gate_low = gate_matrix[layer].astype(jnp.bfloat16)
        feature_row = feature_vectors[layer]
        center, scale = moments(stream)
        unit = (stream - center) * scale
        normed = unit * feature_row[0] + feature_row[1]
        normed_low = normed.astype(jnp.bfloat16)
        drive, states_low = state_forward(normed_low, in_low, state_vectors[layer], masks)
        mixed = (
            jnp.dot(states_low, out_low, preferred_element_type=jnp.float32)
            + feature_row[2] * normed
        )
        act = smooth(mixed)
        act_all = lax.all_gather(act.astype(jnp.bfloat16), "feat", axis=1, tiled=True)
        pre = jnp.dot(act_all, gate_low, preferred_element_type=jnp.float32) + feature_row[3]
        saved.append((scale, unit, normed, normed_low, drive, states_low, mixed, act, act_all, pre))
        stream = stream + act * jax.nn.sigmoid(pre)
    grad = cotangent.astype(jnp.float32) * masks[0][:, None]
    layer_grads = [None] * layers
    for layer in reversed(range(layers)):
        scale, unit, normed, normed_low, drive, states_low, mixed, act, act_all, pre = saved[layer]
        in_low = input_matrix[layer].astype(jnp.bfloat16)
        out_low = output_matrix[layer].astype(jnp.bfloat16)
        gate_low = gate_matrix[layer].astype(jnp.bfloat16)
        feature_row = feature_vectors[layer]
        gate = jax.nn.sigmoid(pre)
        pre_grad = (grad * act * gate * (1.0 - gate)).astype(jnp.bfloat16)
        gate_grad = contract_rows(act_all, pre_grad)
        gate_bias_grad = jnp.sum(pre_grad.astype(jnp.float32), 0)
        act_grad = grad * gate + lax.psum_scatter(
            contract_cols(pre_grad, gate_low), "feat", scatter_dimension=1, tiled=True
        )
        mixed_grad = jax.vjp(smooth, mixed)[1](act_grad)[0]
        skip_grad = jnp.sum(mixed_grad * normed, 0)
        mixed_low = mixed_grad.astype(jnp.bfloat16)
        out_grad = contract_rows(states_low, mixed_low)
        drive_low, row_grad = state_backward(drive, state_vectors[layer], masks, mixed_low, out_low)
        in_grad = contract_rows(normed_low, drive_low)
        normed_grad = mixed_grad * feature_row[2] + contract_cols(drive_low, in_low)
        gain_grad = jnp.sum(normed_grad * unit, 0)
        bias_grad = jnp.sum(normed_grad, 0)
        unit_grad = normed_grad * feature_row[0]
        first_mean, second_mean = back_moments(unit_grad, unit)
        grad = grad + scale * (unit_grad - first_mean - unit * second_mean)
        feature_grad = jnp.stack([gain_grad, bias_grad, skip_grad, gate_bias_grad])
        layer_grads[layer] = (in_grad, out_grad, gate_grad, feature_grad, row_grad)
    stacked_in = jnp.stack([entry[0] for entry in layer_grads])
    stacked_out = jnp.stack([entry[1] for entry in layer_grads])
    stacked_gate = jnp.stack([entry[2] for entry in layer_grads])
    stacked_feature = jnp.stack([entry[3] for entry in layer_grads])
    stacked_state = jnp.stack([entry[4] for entry in layer_grads])
    summed = lax.psum(
        (stacked_in, stacked_out, stacked_gate, stacked_feature, stacked_state), "seq"
    )
    factor = 1.0 / math.sqrt(count * lax.axis_size("seq"))
    grad_in = summed[0] * factor
    grad_out = summed[1] * factor
    grad_gate = summed[2] * factor
    grad_feature = summed[3] * factor
    grad_state = summed[4] * factor
    new_in = update(input_matrix, grad_in, velocity_input, average_input, slow_rate, 0.0)
    new_out = update(output_matrix, grad_out, velocity_output, average_output, slow_rate, 0.0)
    new_gate = update(gate_matrix, grad_gate, velocity_gate, average_gate, main_rate, weight_decay)
    new_feature = update(
        feature_vectors, grad_feature, velocity_feature, average_feature, main_rate, weight_decay
    )
    new_state = update(state_vectors, grad_state, velocity_state, average_state, slow_rate, 0.0)
    return (
        stream,
        grad,
        grad_in,
        grad_out,
        grad_gate,
        grad_feature,
        grad_state,
        new_in[0],
        new_out[0],
        new_gate[0],
        new_feature[0],
        new_state[3],
        new_in[1],
        new_out[1],
        new_gate[1],
        new_feature[1],
        new_state[1],
        new_in[2],
        new_out[2],
        new_gate[2],
        new_feature[2],
        new_state[2],
    )


def solution(mesh):
    return jax.shard_map(
        body,
        mesh=mesh,
        in_specs=(
            P("seq", "feat"),
            P("seq", "feat"),
            P("seq"),
            P("seq"),
            P(None, "feat", None),
            P(None, None, "feat"),
            P(None, None, "feat"),
            P(None, None, "feat"),
            P(),
            P(None, "feat", None),
            P(None, None, "feat"),
            P(None, None, "feat"),
            P(None, None, "feat"),
            P(),
            P(None, "feat", None),
            P(None, None, "feat"),
            P(None, None, "feat"),
            P(None, None, "feat"),
            P(),
        ),
        out_specs=(
            P("seq", "feat"),
            P("seq", "feat"),
            P(None, "feat", None),
            P(None, None, "feat"),
            P(None, None, "feat"),
            P(None, None, "feat"),
            P(),
            P(None, "feat", None),
            P(None, None, "feat"),
            P(None, None, "feat"),
            P(None, None, "feat"),
            P(),
            P(None, "feat", None),
            P(None, None, "feat"),
            P(None, None, "feat"),
            P(None, None, "feat"),
            P(),
            P(None, "feat", None),
            P(None, None, "feat"),
            P(None, None, "feat"),
            P(None, None, "feat"),
            P(),
        ),
        check_vma=False,
    )
```

profile of v0, /device:TPU:0, one launch (start us, length us, event | category | flops | bytes accessed | tf_op | source)
XLA Modules:
  0.0 1222.3 jit_solution(16966885579422786372)
XLA Ops:
  10.5 22.2 %all-gather.7.cloned.1.call-done = f32[768,512]{1,0:T(8,128)} async-done(((f32[768,128]{1,0:T(8,128)}), f32[768,512]{1,0:T(8,128)}) %all-gather.7.cloned.1.call-update) | async-done | bytes 1572880 | tf_op jit(solution)/shard_map/all_gather | solution.py:108
  36.7 3.1 fusion.344
  43.4 52.2 %all-reduce.322.cloned.1.call-done = f32[768,768]{1,0:T(8,128)} async-done(((f32[768,768]{1,0:T(8,128)}), f32[768,768]{1,0:T(8,128)}) %all-reduce.322.cloned.1.call-update) | async-done | bytes 2359312 | tf_op jit(solution)/shard_map/psum | solution.py:125
  103.3 2.9 subtract_add_fusion.23
  154.0 8.2 all_gather.25
  164.5 20.4 %all-gather.9.cloned.1.call-done = f32[768,512]{1,0:T(8,128)} async-done(((f32[768,128]{1,0:T(8,128)}), f32[768,512]{1,0:T(8,128)}) %all-gather.9.cloned.1.call-update) | async-done | bytes 1572880 | tf_op jit(solution)/shard_map/all_gather | solution.py:108
  188.8 3.1 fusion.345
  192.1 55.7 %all-reduce.324.cloned.1.call-done = f32[768,768]{1,0:T(8,128)} async-done(((f32[768,768]{1,0:T(8,128)}), f32[768,768]{1,0:T(8,128)}) %all-reduce.324.cloned.1.call-update) | async-done | bytes 2359312 | tf_op jit(solution)/shard_map/psum | solution.py:125
  256.6 3.1 subtract_add_fusion.11
  306.8 8.2 all_gather.27
  314.9 2.7 convert_reduce_fusion
  320.8 28.8 %reduce-scatter.3.cloned.1.call-done = f32[768,128]{1,0:T(8,128)} async-done(((f32[768,512]{1,0:T(8,128)}), f32[768,128]{1,0:T(8,128)}) %reduce-scatter.3.cloned.1.call-update) | async-done | bytes 393232 | tf_op jit(solution)/shard_map/reduce_scatter | solution.py:199
  352.9 3.9 fusion.341
  357.1 93.9 %all-reduce.326.cloned.1.call-done = f32[768,1536]{1,0:T(8,128)} async-done(((f32[768,1536]{1,0:T(8,128)}), f32[768,1536]{1,0:T(8,128)}) %all-reduce.326.cloned.1.call-update) | async-done | bytes 4718608 | tf_op jit(solution)/shard_map/psum | solution.py:136
  451.0 5.1 fusion.478
  456.1 2.9 fusion.328
  461.9 5.8 fusion.447
  467.7 3.6 fusion.502
  484.1 3.0 fusion.433
  494.6 4.0 fusion.445
  506.1 3.8 fusion.444
  517.8 4.0 fusion.432
  528.8 4.2 fusion.431
  541.2 3.4 fusion.443
  550.6 3.4 fusion.442
  562.2 3.8 fusion.430
  574.6 3.8 fusion.429
  586.3 4.0 fusion.441
  590.3 2.9 fusion.497
  599.9 4.0 fusion.440
  611.9 3.9 fusion.439
  622.0 3.7 multiply_reduce_fusion.3
  629.3 3.4 fusion.428
  645.8 3.5 multiply_reduce_fusion.2
  655.9 2.9 multiply_reduce_fusion.19
  659.7 19.4 %all-gather.13.cloned.1.call-done = f32[768,512]{1,0:T(8,128)} async-done(((f32[768,128]{1,0:T(8,128)}), f32[768,512]{1,0:T(8,128)}) %all-gather.13.cloned.1.call-update) | async-done | bytes 1572880 | tf_op jit(solution)/shard_map/all_gather | solution.py:118
  680.7 20.4 %all-gather.11.cloned.1.call-done = f32[768,512]{1,0:T(8,128)} async-done(((f32[768,128]{1,0:T(8,128)}), f32[768,512]{1,0:T(8,128)}) %all-gather.11.cloned.1.call-update) | async-done | bytes 1572880 | tf_op jit(solution)/shard_map/all_gather | solution.py:117
  707.7 28.3 %reduce-scatter.5.cloned.1.call-done = f32[768,128]{1,0:T(8,128)} async-done(((f32[768,512]{1,0:T(8,128)}), f32[768,128]{1,0:T(8,128)}) %reduce-scatter.5.cloned.1.call-update) | async-done | bytes 393232 | tf_op jit(solution)/shard_map/reduce_scatter | solution.py:199
  737.9 3.9 fusion.340
  742.3 93.7 %all-reduce.328.cloned.1.call-done = f32[768,1536]{1,0:T(8,128)} async-done(((f32[768,1536]{1,0:T(8,128)}), f32[768,1536]{1,0:T(8,128)}) %all-reduce.328.cloned.1.call-update) | async-done | bytes 4718608 | tf_op jit(solution)/shard_map/psum | solution.py:136
  836.0 4.8 fusion.477
  840.8 2.9 fusion.324
  846.5 5.0 fusion.423
  851.6 3.6 fusion.486
  867.6 3.4 fusion.409
  876.8 3.2 fusion.421
  885.6 3.4 fusion.420
  894.9 3.6 fusion.408
  904.8 3.9 fusion.407
  916.5 3.8 fusion.419
  928.0 3.8 fusion.418
  940.1 3.8 fusion.406
  952.5 3.9 fusion.405
  964.5 4.0 fusion.417
  968.5 2.9 fusion.481
  978.2 4.0 fusion.416
  990.1 3.9 fusion.415
  1000.2 3.0 multiply_reduce_fusion.11
  1006.9 3.4 fusion.404
  1023.3 2.9 multiply_reduce_fusion.10
  1032.8 2.9 multiply_reduce_fusion.21
  1049.8 37.1 %all-reduce.314 = (f32[2,4,128]{2,1,0:T(4,128)S(1)}, f32[2,3,384]{2,1,0:T(4,128)S(1)}) all-reduce(f32[2,4,128]{2,1,0:T(4,128)S(1)} %pad_maximum_fusion.10, f32[2,3,384]{2,1,0:T(4,128)S(1)} %pad_maximum_fusion.9), channel_id=1, replica_groups=mesh['seq'=8,'feat'=4] {'seq'}, use_global_device_ids=true, to_apply=%region_28.0 | all-reduce | flops 3328 | bytes 26624 | tf_op jit(solution)/shard_map/psum | solution.py:221
  1095.4 110.1 %all-reduce.330.cloned.1.call-done = (f32[2,128,768]{2,1,0:T(8,128)}, f32[2,1536,128]{2,1,0:T(8,128)}, f32[2,512,128]{2,1,0:T(8,128)}) async-done(((f32[2,128,768]{2,1,0:T(8,128)}, f32[2,1536,128]{2,1,0:T(8,128)}, f32[2,512,128]{2,1,0:T(8,128)}), (f32[2,128,768]{2,1,0:T(8,128)}, f32[2,1536,128]{2,1,0:T(8,128)}, f32[2,512,128]{2,1,0:T(8,128)})) %all-reduce.330.cloned.1.call-update) | async-done | bytes 2883600 | tf_op jit(solution)/shard_map/psum | solution.py:221
  1212.2 3.1 add_multiply_fusion
  (1597 shorter events, 422.5 us)
Async XLA Ops:
  7.2 25.5 %all-gather.7.cloned.1.call-start = ((), (), s32[]{:S(2)}) async-start(), calls=%async_computation.2 | async-start | bytes 1966080 | tf_op jit(solution)/shard_map/all_gather | solution.py:108
  9.0 86.5 %all-reduce.322.cloned.1.call-start = ((), (), s32[]{:S(2)}) async-start(), calls=%async_computation.3 | async-start | bytes 4718592 | tf_op jit(solution)/shard_map/psum | solution.py:125
  39.8 145.1 %all-gather.9.cloned.1.call-start = ((), (), s32[]{:S(2)}) async-start(), calls=%async_computation.4 | async-start | bytes 1966080 | tf_op jit(solution)/shard_map/all_gather | solution.py:108
  43.4 54.2 %copy-start.553 = (f32[384]{0:T(512)}, f32[384]{0:T(512)S(1)}, u32[]{:S(2)}) copy-start(f32[384]{0:T(512)S(1)} %get-tuple-element.706) | copy-start | bytes 4612
  43.4 54.2 %copy-start.555 = (f32[384]{0:T(512)}, f32[384]{0:T(512)S(1)}, u32[]{:S(2)}) copy-start(f32[384]{0:T(512)S(1)} %get-tuple-element.707) | copy-start | bytes 4612
  100.3 27.3 %copy-start.16 = (f32[768,384]{1,0:T(8,128)}, f32[768,384]{1,0:T(8,128)S(1)}, u32[]{:S(2)}) copy-start(f32[768,384]{1,0:T(8,128)S(1)} %get-tuple-element.600) | copy-start | bytes 3538948
  100.3 27.3 %copy-start.20 = (f32[768,384]{1,0:T(8,128)}, f32[768,384]{1,0:T(8,128)S(1)}, u32[]{:S(2)}) copy-start(f32[768,384]{1,0:T(8,128)S(1)} %get-tuple-element.599) | copy-start | bytes 3538948
  100.4 5.9 copy-start.122
  100.5 5.8 copy-start.124
  106.2 21.8 %copy-start = (f32[768,384]{1,0:T(8,128)}, f32[768,384]{1,0:T(8,128)S(1)}, u32[]{:S(2)}) copy-start(f32[768,384]{1,0:T(8,128)S(1)} %get-tuple-element.376) | copy-start | bytes 3538948
  106.2 21.8 %copy-start.2 = (f32[768,384]{1,0:T(8,128)}, f32[768,384]{1,0:T(8,128)S(1)}, u32[]{:S(2)}) copy-start(f32[768,384]{1,0:T(8,128)S(1)} %get-tuple-element.377) | copy-start | bytes 3538948
  106.2 22.6 %copy-start.24 = (f32[768,384]{1,0:T(8,128)}, f32[768,384]{1,0:T(8,128)S(1)}, u32[]{:S(2)}) copy-start(f32[768,384]{1,0:T(8,128)S(1)} %get-tuple-element.375) | copy-start | bytes 3538948
  125.3 19.5 %copy-start.148 = (f32[768,384]{1,0:T(8,128)}, f32[768,384]{1,0:T(8,128)S(1)}, u32[]{:S(2)}) copy-start(f32[768,384]{1,0:T(8,128)S(1)} %get-tuple-element.382) | copy-start | bytes 3538948
  125.4 19.5 %copy-start.150 = (f32[768,384]{1,0:T(8,128)}, f32[768,384]{1,0:T(8,128)S(1)}, u32[]{:S(2)}) copy-start(f32[768,384]{1,0:T(8,128)S(1)} %get-tuple-element.383) | copy-start | bytes 3538948
  143.9 5.4 copy-start.152
  143.9 5.4 copy-start.154
  143.9 5.3 copy-start.403
  153.9 10.5 copy-start.521
  154.0 10.5 copy-start.523
  164.4 83.3 %all-reduce.324.cloned.1.call-start = ((), (), s32[]{:S(2)}) async-start(), calls=%async_computation.5 | async-start | bytes 4718592 | tf_op jit(solution)/shard_map/psum | solution.py:125
  192.0 157.6 %reduce-scatter.3.cloned.1.call-start = ((), (), s32[]{:S(2)}) async-start(), calls=%async_computation.6 | async-start | bytes 1966080 | tf_op jit(solution)/shard_map/reduce_scatter | solution.py:199
  192.1 57.7 %copy-start.557 = (f32[384]{0:T(512)}, f32[384]{0:T(512)S(1)}, u32[]{:S(2)}) copy-start(f32[384]{0:T(512)S(1)} %get-tuple-element.700) | copy-start | bytes 4612
  192.1 57.7 %copy-start.559 = (f32[384]{0:T(512)}, f32[384]{0:T(512)S(1)}, u32[]{:S(2)}) copy-start(f32[384]{0:T(512)S(1)} %get-tuple-element.701) | copy-start | bytes 4612
  253.7 27.3 %copy-start.18 = (f32[768,384]{1,0:T(8,128)}, f32[768,384]{1,0:T(8,128)S(1)}, u32[]{:S(2)}) copy-start(f32[768,384]{1,0:T(8,128)S(1)} %get-tuple-element.602) | copy-start | bytes 3538948
  253.7 27.3 %copy-start.22 = (f32[768,384]{1,0:T(8,128)}, f32[768,384]{1,0:T(8,128)S(1)}, u32[]{:S(2)}) copy-start(f32[768,384]{1,0:T(8,128)S(1)} %get-tuple-element.601) | copy-start | bytes 3538948
  253.8 6.2 copy-start.126
  253.9 6.1 copy-start.128
  259.8 21.5 %copy-start.4 = (f32[768,384]{1,0:T(8,128)}, f32[768,384]{1,0:T(8,128)S(1)}, u32[]{:S(2)}) copy-start(f32[768,384]{1,0:T(8,128)S(1)} %get-tuple-element.320) | copy-start | bytes 3538948
  259.8 21.5 %copy-start.6 = (f32[768,384]{1,0:T(8,128)}, f32[768,384]{1,0:T(8,128)S(1)}, u32[]{:S(2)}) copy-start(f32[768,384]{1,0:T(8,128)S(1)} %get-tuple-element.321) | copy-start | bytes 3538948
  259.8 22.4 %copy-start.30 = (f32[768,384]{1,0:T(8,128)}, f32[768,384]{1,0:T(8,128)S(1)}, u32[]{:S(2)}) copy-start(f32[768,384]{1,0:T(8,128)S(1)} %get-tuple-element.319) | copy-start | bytes 3538948
  278.7 19.5 %copy-start.156 = (f32[768,384]{1,0:T(8,128)}, f32[768,384]{1,0:T(8,128)S(1)}, u32[]{:S(2)}) copy-start(f32[768,384]{1,0:T(8,128)S(1)} %get-tuple-element.326) | copy-start | bytes 3538948
  278.7 19.5 %copy-start.158 = (f32[768,384]{1,0:T(8,128)}, f32[768,384]{1,0:T(8,128)S(1)}, u32[]{:S(2)}) copy-start(f32[768,384]{1,0:T(8,128)S(1)} %get-tuple-element.327) | copy-start | bytes 3538948
  304.1 10.8 copy-start.529
  304.1 10.8 copy-start.589
  306.7 10.9 copy-start.549
  306.8 10.9 copy-start.550
  320.8 130.2 %all-reduce.326.cloned.1.call-start = ((), (), s32[]{:S(2)}) async-start(), calls=%async_computation.7 | async-start | bytes 9437184 | tf_op jit(solution)/shard_map/psum | solution.py:136
  356.8 322.2 %all-gather.13.cloned.1.call-start = ((), (), s32[]{:S(2)}) async-start(), calls=%async_computation.9 | async-start | bytes 1966080 | tf_op jit(solution)/shard_map/all_gather | solution.py:118
  451.0 9.3 copy-start.251
  467.7 5.1 copy-start.506
  471.3 18.4 %copy-start.349 = (f32[768,384]{1,0:T(8,128)}, f32[768,384]{1,0:T(8,128)S(1)}, u32[]{:S(2)}) copy-start(f32[768,384]{1,0:T(8,128)S(1)} %get-tuple-element.654) | copy-start | bytes 3538948
  658.9 42.2 %all-gather.11.cloned.1.call-start = ((), (), s32[]{:S(2)}) async-start(), calls=%async_computation.8 | async-start | bytes 1966080 | tf_op jit(solution)/shard_map/all_gather | solution.py:117
  659.6 76.4 %reduce-scatter.5.cloned.1.call-start = ((), (), s32[]{:S(2)}) async-start(), calls=%async_computation.10 | async-start | bytes 1966080 | tf_op jit(solution)/shard_map/reduce_scatter | solution.py:199
  679.0 23.7 %copy-start.530 = (bf16[768,128]{1,0:T(8,128)(2,1)S(1)}, bf16[768,128]{1,0:T(8,128)(2,1)}, u32[]{:S(2)}) copy-start(bf16[768,128]{1,0:T(8,128)(2,1)} %param.20) | copy-start | bytes 589828
  680.6 22.1 %copy-start.497 = (f32[768,128]{1,0:T(8,128)S(1)}, f32[768,128]{1,0:T(8,128)}, u32[]{:S(2)}) copy-start(f32[768,128]{1,0:T(8,128)} %get-tuple-element.682) | copy-start | bytes 1179652
  680.7 22.1 %copy-start.522 = (f32[768,128]{1,0:T(8,128)S(1)}, f32[768,128]{1,0:T(8,128)}, u32[]{:S(2)}) copy-start(f32[768,128]{1,0:T(8,128)} %copy-done.521) | copy-start | bytes 1179652
  680.7 22.1 %copy-start.524 = (f32[768,128]{1,0:T(8,128)S(1)}, f32[768,128]{1,0:T(8,128)}, u32[]{:S(2)}) copy-start(f32[768,128]{1,0:T(8,128)} %copy-done.523) | copy-start | bytes 1179652
  680.7 22.1 %copy-start.525 = (f32[768,128]{1,0:T(8,128)S(1)}, f32[768,128]{1,0:T(8,128)}, u32[]{:S(2)}) copy-start(f32[768,128]{1,0:T(8,128)} %get-tuple-element.727) | copy-start | bytes 1179652
  704.6 31.4 %copy-start.498 = (f32[768,128]{1,0:T(8,128)}, f32[768,128]{1,0:T(8,128)S(1)}, u32[]{:S(2)}) copy-start(f32[768,128]{1,0:T(8,128)S(1)} %get-tuple-element.286) | copy-start | bytes 1179652
  707.7 128.3 %all-reduce.328.cloned.1.call-start = ((), (), s32[]{:S(2)}) async-start(), calls=%async_computation.11 | async-start | bytes 9437184 | tf_op jit(solution)/shard_map/psum | solution.py:136
  741.8 94.2 %copy-start.450 = (f32[256,384]{1,0:T(8,128)S(1)}, f32[256,384]{1,0:T(8,128)}, u32[]{:S(2)}) copy-start(f32[256,384]{1,0:T(8,128)} %copy-done.449) | copy-start | bytes 1179652
  741.8 94.2 %copy-start.452 = (f32[256,384]{1,0:T(8,128)S(1)}, f32[256,384]{1,0:T(8,128)}, u32[]{:S(2)}) copy-start(f32[256,384]{1,0:T(8,128)} %copy-done.451) | copy-start | bytes 1179652
  741.8 348.1 %all-gather.17.cloned.1.call-start = ((), (), s32[]{:S(2)}) async-start(), calls=%async_computation.13 | async-start | bytes 1966080 | tf_op jit(solution)/shard_map/all_gather | solution.py:118
  836.0 8.8 copy-start.247
  1035.7 55.9 %all-gather.15.cloned.1.call-start = ((), (), s32[]{:S(2)}) async-start(), calls=%async_computation.12 | async-start | bytes 1966080 | tf_op jit(solution)/shard_map/all_gather | solution.py:117
  1036.3 169.1 %all-reduce.330.cloned.1.call-start = ((), (), s32[]{:S(2)}) async-start(), calls=%async_computation.14 | async-start | bytes 5767168 | tf_op jit(solution)/shard_map/psum | solution.py:221
  1048.5 38.4 %copy-start.563 = (f32[2,3,384]{2,0,1:T(2,128)S(1)}, f32[2,3,384]{2,0,1:T(2,128)}, u32[]{:S(2)}) copy-start(f32[2,3,384]{2,0,1:T(2,128)} %param.37) | copy-start | bytes 27652
  1048.5 38.4 %copy-start.564 = (f32[2,3,384]{2,0,1:T(2,128)S(1)}, f32[2,3,384]{2,0,1:T(2,128)}, u32[]{:S(2)}) copy-start(f32[2,3,384]{2,0,1:T(2,128)} %param.32) | copy-start | bytes 27652
  1048.5 40.8 %copy-start.562 = (f32[2,4,128]{2,1,0:T(4,128)S(1)}, f32[2,4,128]{2,1,0:T(4,128)}, u32[]{:S(2)}) copy-start(f32[2,4,128]{2,1,0:T(4,128)} %param.26) | copy-start | bytes 12292
  1048.5 40.8 %copy-start.577 = (f32[2,4,128]{2,1,0:T(4,128)S(1)}, f32[2,4,128]{2,1,0:T(4,128)}, u32[]{:S(2)}) copy-start(f32[2,4,128]{2,1,0:T(4,128)} %param.36) | copy-start | bytes 12292
  1048.5 40.8 %copy-start.578 = (f32[2,4,128]{2,1,0:T(4,128)S(1)}, f32[2,4,128]{2,1,0:T(4,128)}, u32[]{:S(2)}) copy-start(f32[2,4,128]{2,1,0:T(4,128)} %param.31) | copy-start | bytes 12292
  1091.6 113.9 %copy-start.515 = (f32[2,512,128]{2,1,0:T(8,128)S(1)}, f32[2,512,128]{2,1,0:T(8,128)}, u32[]{:S(2)}) copy-start(f32[2,512,128]{2,1,0:T(8,128)} %param.25) | copy-start | bytes 1572868
  1091.6 113.9 %copy-start.547 = (f32[2,512,128]{2,1,0:T(8,128)S(1)}, f32[2,512,128]{2,1,0:T(8,128)}, u32[]{:S(2)}) copy-start(f32[2,512,128]{2,1,0:T(8,128)} %param.35) | copy-start | bytes 1572868
  1091.6 113.9 %copy-start.548 = (f32[2,512,128]{2,1,0:T(8,128)S(1)}, f32[2,512,128]{2,1,0:T(8,128)}, u32[]{:S(2)}) copy-start(f32[2,512,128]{2,1,0:T(8,128)} %param.30) | copy-start | bytes 1572868
  (541 other events, 1082.5 us)
Sparse Core Ops, SparseCore 0:
  10.2 22.5 all-gather.6
  39.9 55.6 all-reduce.321
  164.6 20.2 all-gather.8
  192.1 55.6 all-reduce.323
  320.9 28.6 reduce-scatter.2
  356.9 94.0 all-reduce.325
  659.0 19.9 all-gather.12
  681.2 19.8 all-gather.10
  707.8 28.1 reduce-scatter.4
  742.0 94.0 all-reduce.327
  1035.9 19.9 all-gather.16
  1057.9 19.8 all-gather.14
  1082.3 123.1 all-reduce.329
where the time goes:
time: 1230 us; the launch traced here: 1220 us
  waiting for transfers between devices  546 us (44%)
  other arithmetic  391 us (32%)
  local copies, waits for them, and re-layouts  167 us (14%)
  blocking collectives  53.4 us (4%)
  matrix products  42.7 us (3%)
  between operations  20.4 us (2%)
    psum x2, waiting for transfers between devices, state_backward(): states_grad = lax.psum(partial_states, 'feat')  188 us
    unnamed x1188, local copies, waits for them, and re-layouts  153 us
    neg x32, other arithmetic, combine(): mult_real = later[0] * earlier[0] - later[1] * earlier[1]  115 us
    psum x1, waiting for transfers between devices, body(): lax.psum((stacked_in, stacked_out, stacked_gate, stacked_feature, stacked...  110 us
    psum x2, waiting for transfers between devices, state_forward(): drive = lax.psum(partial_drive, 'feat')  108 us
    add_any x40, other arithmetic, combine(): add_real = later[0] * earlier[2] - later[1] * earlier[3] + later[2]  59.8 us
    neg x36, other arithmetic, combine(): add_real = later[0] * earlier[2] - later[1] * earlier[3] + later[2]  58.3 us
    reduce_scatter x2, waiting for transfers between devices, body(): lax.psum_scatter(contract_cols(pre_grad, gate_low), 'feat', scatter_dimen...  57 us
  transfers between devices with their start and end apart: 13, of which 11 were waited for; matrix products, arithmetic and copies ran while one was open for 2% of the time, Pallas kernels for 0%

commit v1 on v0

--- a/solution.py
+++ b/solution.py
@@ -105,7 +105,9 @@
 
 
 def moments(stream):
-    whole = lax.all_gather(stream, "feat", axis=1, tiled=True)
+    whole = jnp.concatenate(
+        lax.all_to_all(jnp.stack([stream] * lax.axis_size("feat")), "feat", 0, 0), axis=1
+    )
     center = jnp.mean(whole, 1, keepdims=True)
     spread = whole - center
     variance = jnp.mean(spread * spread, 1, keepdims=True)

time: 1230 us -> 1230 us (level)
  blocking collectives: 53.4 us -> 75.9 us
  waiting for transfers between devices: 546 us -> 524 us
    all_gather x2 -> x0, waiting for transfers between devices: 42.6 us -> none  [moments(): whole = lax.all_gather(stream, 'feat', axis=1, tiled=True)]
    all_to_all x0 -> x1, blocking collectives: none -> 22.5 us  [moments(): lax.all_to_all(jnp.stack([stream] * lax.axis_size('feat')), 'feat', 0, 0)]
    all_to_all x0 -> x1, waiting for transfers between devices: none -> 18.7 us  [moments(): lax.all_to_all(jnp.stack([stream] * lax.axis_size('feat')), 'feat', 0, 0)]
    unnamed x1188 -> x1184, local copies, waits for them, and re-layouts: 153 us -> 153 us
  transfers between devices with their start and end apart: 13 -> 12, of which waited for: 11 -> 10; matrix products, arithmetic and copies ran while one was open for 2% -> 2% of each run, Pallas kernels for 0% -> 0%
where the time goes in v1:
time: 1230 us; the launch traced here: 1220 us
  waiting for transfers between devices  524 us (43%)
  other arithmetic  386 us (31%)
  local copies, waits for them, and re-layouts  169 us (14%)
  blocking collectives  75.9 us (6%)
  matrix products  42.6 us (3%)
  between operations  20.2 us (2%)
    psum x2, waiting for transfers between devices, state_backward(): states_grad = lax.psum(partial_states, 'feat')  188 us
    unnamed x1184, local copies, waits for them, and re-layouts  153 us
    neg x32, other arithmetic, combine(): mult_real = later[0] * earlier[0] - later[1] * earlier[1]  115 us
    psum x1, waiting for transfers between devices, body(): lax.psum((stacked_in, stacked_out, stacked_gate, stacked_feature, stacked...  110 us
    psum x2, waiting for transfers between devices, state_forward(): drive = lax.psum(partial_drive, 'feat')  109 us
    add_any x40, other arithmetic, combine(): add_real = later[0] * earlier[2] - later[1] * earlier[3] + later[2]  59.9 us
    neg x36, other arithmetic, combine(): add_real = later[0] * earlier[2] - later[1] * earlier[3] + later[2]  58.3 us
    reduce_scatter x2, waiting for transfers between devices, body(): lax.psum_scatter(contract_cols(pre_grad, gate_low), 'feat', scatter_dimen...  57 us
  transfers between devices with their start and end apart: 12, of which 10 were waited for; matrix products, arithmetic and copies ran while one was open for 2% of the time, Pallas kernels for 0%

profile of v1, /device:TPU:0, one launch (start us, length us, event | category | flops | bytes accessed | tf_op | source)
XLA Modules:
  0.0 1222.6 jit_solution(17021295266570212307)
XLA Ops:
  9.4 4.3 all-to-all-start
  15.1 18.7 %all-to-all-done = f32[4,768,128]{2,1,0:T(8,128)S(1)} async-done(((f32[4,768,128]{2,1,0:T(8,128)}), f32[4,768,128]{2,1,0:T(8,128)S(1)}, u32[]{:S(2)}, u32[]{:S(2)}) %all-to-all-start) | async-done | bytes 1572896 | tf_op jit(solution)/shard_map/all_to_all | solution.py:109
  36.2 3.1 fusion.344
  42.9 53.3 %all-reduce.322.cloned.1.call-done = f32[768,768]{1,0:T(8,128)} async-done(((f32[768,768]{1,0:T(8,128)}), f32[768,768]{1,0:T(8,128)}) %all-reduce.322.cloned.1.call-update) | async-done | bytes 2359312 | tf_op jit(solution)/shard_map/psum | solution.py:127
  103.9 2.9 subtract_add_fusion.23
  154.4 8.2 all_gather.18
  164.8 22.5 %all_to_all.10 = f32[4,768,128]{2,1,0:T(8,128)S(1)} all-to-all(f32[4,768,128]{2,1,0:T(8,128)S(1)} %stack.90), channel_id=1, replica_groups=mesh['seq'=8,'feat'=4] {'feat'}, dimensions={0} | all-to-all | bytes 3145728 | tf_op jit(solution)/shard_map/all_to_all | solution.py:109
  189.8 3.1 fusion.345
  193.0 55.7 %all-reduce.324.cloned.1.call-done = f32[768,768]{1,0:T(8,128)} async-done(((f32[768,768]{1,0:T(8,128)}), f32[768,768]{1,0:T(8,128)}) %all-reduce.324.cloned.1.call-update) | async-done | bytes 2359312 | tf_op jit(solution)/shard_map/psum | solution.py:127
  257.5 2.9 subtract_add_fusion.11
  307.4 8.2 all_gather.19
  321.5 28.7 %reduce-scatter.3.cloned.1.call-done = f32[768,128]{1,0:T(8,128)} async-done(((f32[768,512]{1,0:T(8,128)}), f32[768,128]{1,0:T(8,128)}) %reduce-scatter.3.cloned.1.call-update) | async-done | bytes 393232 | tf_op jit(solution)/shard_map/reduce_scatter | solution.py:201
  353.6 3.9 fusion.341
  357.9 93.7 %all-reduce.326.cloned.1.call-done = f32[768,1536]{1,0:T(8,128)} async-done(((f32[768,1536]{1,0:T(8,128)}), f32[768,1536]{1,0:T(8,128)}) %all-reduce.326.cloned.1.call-update) | async-done | bytes 4718608 | tf_op jit(solution)/shard_map/psum | solution.py:138
  451.6 5.1 fusion.478
  456.8 2.9 fusion.328
  462.6 5.8 fusion.447
  468.4 3.6 fusion.502
  484.7 3.0 fusion.433
  495.2 4.0 fusion.445
  506.8 3.8 fusion.444
  518.4 4.0 fusion.432
  529.4 3.9 fusion.431
  541.5 3.4 fusion.443
  550.9 3.4 fusion.442
  562.5 3.8 fusion.430
  574.9 3.8 fusion.429
  586.6 4.0 fusion.441
  590.6 2.9 fusion.497
  600.2 4.0 fusion.440
  612.2 3.9 fusion.439
  622.3 3.8 multiply_reduce_fusion.3
  629.8 3.4 fusion.428
  646.3 3.5 multiply_reduce_fusion.2
  656.4 2.9 multiply_reduce_fusion.19
  660.0 19.5 %all-gather.7.cloned.1.call-done = f32[768,512]{1,0:T(8,128)} async-done(((f32[768,128]{1,0:T(8,128)}), f32[768,512]{1,0:T(8,128)}) %all-gather.7.cloned.1.call-update) | async-done | bytes 1572880 | tf_op jit(solution)/shard_map/all_gather | solution.py:120
  681.2 20.2 %all-gather.5.cloned.1.call-done = f32[768,512]{1,0:T(8,128)} async-done(((f32[768,128]{1,0:T(8,128)}), f32[768,512]{1,0:T(8,128)}) %all-gather.5.cloned.1.call-update) | async-done | bytes 1572880 | tf_op jit(solution)/shard_map/all_gather | solution.py:119
  708.1 28.3 %reduce-scatter.5.cloned.1.call-done = f32[768,128]{1,0:T(8,128)} async-done(((f32[768,512]{1,0:T(8,128)}), f32[768,128]{1,0:T(8,128)}) %reduce-scatter.5.cloned.1.call-update) | async-done | bytes 393232 | tf_op jit(solution)/shard_map/reduce_scatter | solution.py:201
  738.3 3.9 fusion.340
  742.4 93.9 %all-reduce.328.cloned.1.call-done = f32[768,1536]{1,0:T(8,128)} async-done(((f32[768,1536]{1,0:T(8,128)}), f32[768,1536]{1,0:T(8,128)}) %all-reduce.328.cloned.1.call-update) | async-done | bytes 4718608 | tf_op jit(solution)/shard_map/psum | solution.py:138
  836.4 4.8 fusion.477
  841.2 2.9 fusion.324
  846.9 5.0 fusion.423
  851.9 3.6 fusion.486
  867.9 3.4 fusion.409
  877.1 3.2 fusion.421
  885.9 3.4 fusion.420
  895.2 3.6 fusion.408
  905.2 4.1 fusion.407
  917.1 3.8 fusion.419
  928.6 3.8 fusion.418
  940.7 3.8 fusion.406
  953.1 3.9 fusion.405
  965.1 4.0 fusion.417
  969.1 2.9 fusion.481
  978.7 4.0 fusion.416
  990.7 3.9 fusion.415
  1000.8 3.0 multiply_reduce_fusion.11
  1007.4 3.4 fusion.404
  1023.9 2.9 multiply_reduce_fusion.10
  1033.4 2.9 multiply_reduce_fusion.21
  1050.3 37.1 %all-reduce.314 = (f32[2,4,128]{2,1,0:T(4,128)S(1)}, f32[2,3,384]{2,1,0:T(4,128)S(1)}) all-reduce(f32[2,4,128]{2,1,0:T(4,128)S(1)} %pad_maximum_fusion.10, f32[2,3,384]{2,1,0:T(4,128)S(1)} %pad_maximum_fusion.9), channel_id=1, replica_groups=mesh['seq'=8,'feat'=4] {'seq'}, use_global_device_ids=true, to_apply=%region_28.0 | all-reduce | flops 3328 | bytes 26624 | tf_op jit(solution)/shard_map/psum | solution.py:223
  1095.8 110.2 %all-reduce.330.cloned.1.call-done = (f32[2,128,768]{2,1,0:T(8,128)}, f32[2,1536,128]{2,1,0:T(8,128)}, f32[2,512,128]{2,1,0:T(8,128)}) async-done(((f32[2,128,768]{2,1,0:T(8,128)}, f32[2,1536,128]{2,1,0:T(8,128)}, f32[2,512,128]{2,1,0:T(8,128)}), (f32[2,128,768]{2,1,0:T(8,128)}, f32[2,1536,128]{2,1,0:T(8,128)}, f32[2,512,128]{2,1,0:T(8,128)})) %all-reduce.330.cloned.1.call-update) | async-done | bytes 2883600 | tf_op jit(solution)/shard_map/psum | solution.py:223
  1212.8 3.1 add_multiply_fusion
  (1591 shorter events, 421.8 us)
Async XLA Ops:
  9.4 24.4 %all-to-all-start = ((f32[4,768,128]{2,1,0:T(8,128)}), f32[4,768,128]{2,1,0:T(8,128)S(1)}, u32[]{:S(2)}, u32[]{:S(2)}) async-start(f32[4,768,128]{2,1,0:T(8,128)} %stack.89), calls=%async_computation | async-start | bytes 3145728 | tf_op jit(solution)/shard_map/all_to_all | solution.py:109
  13.7 82.5 %all-reduce.322.cloned.1.call-start = ((), (), s32[]{:S(2)}) async-start(), calls=%async_computation.4 | async-start | bytes 4718592 | tf_op jit(solution)/shard_map/psum | solution.py:127
  39.3 209.4 %all-reduce.324.cloned.1.call-start = ((), (), s32[]{:S(2)}) async-start(), calls=%async_computation.5 | async-start | bytes 4718592 | tf_op jit(solution)/shard_map/psum | solution.py:127
  42.9 55.3 %copy-start.551 = (f32[384]{0:T(512)}, f32[384]{0:T(512)S(1)}, u32[]{:S(2)}) copy-start(f32[384]{0:T(512)S(1)} %get-tuple-element.706) | copy-start | bytes 4612
  42.9 55.3 %copy-start.553 = (f32[384]{0:T(512)}, f32[384]{0:T(512)S(1)}, u32[]{:S(2)}) copy-start(f32[384]{0:T(512)S(1)} %get-tuple-element.707) | copy-start | bytes 4612
  100.9 27.3 %copy-start.16 = (f32[768,384]{1,0:T(8,128)}, f32[768,384]{1,0:T(8,128)S(1)}, u32[]{:S(2)}) copy-start(f32[768,384]{1,0:T(8,128)S(1)} %get-tuple-element.600) | copy-start | bytes 3538948
  100.9 27.3 %copy-start.20 = (f32[768,384]{1,0:T(8,128)}, f32[768,384]{1,0:T(8,128)S(1)}, u32[]{:S(2)}) copy-start(f32[768,384]{1,0:T(8,128)S(1)} %get-tuple-element.599) | copy-start | bytes 3538948
  101.0 5.9 copy-start.122
  101.1 5.8 copy-start.124
  106.8 21.7 %copy-start = (f32[768,384]{1,0:T(8,128)}, f32[768,384]{1,0:T(8,128)S(1)}, u32[]{:S(2)}) copy-start(f32[768,384]{1,0:T(8,128)S(1)} %get-tuple-element.376) | copy-start | bytes 3538948
  106.8 21.7 %copy-start.2 = (f32[768,384]{1,0:T(8,128)}, f32[768,384]{1,0:T(8,128)S(1)}, u32[]{:S(2)}) copy-start(f32[768,384]{1,0:T(8,128)S(1)} %get-tuple-element.377) | copy-start | bytes 3538948
  106.8 22.5 %copy-start.24 = (f32[768,384]{1,0:T(8,128)}, f32[768,384]{1,0:T(8,128)S(1)}, u32[]{:S(2)}) copy-start(f32[768,384]{1,0:T(8,128)S(1)} %get-tuple-element.375) | copy-start | bytes 3538948
  125.9 19.4 %copy-start.148 = (f32[768,384]{1,0:T(8,128)}, f32[768,384]{1,0:T(8,128)S(1)}, u32[]{:S(2)}) copy-start(f32[768,384]{1,0:T(8,128)S(1)} %get-tuple-element.382) | copy-start | bytes 3538948
  125.9 19.4 %copy-start.150 = (f32[768,384]{1,0:T(8,128)}, f32[768,384]{1,0:T(8,128)S(1)}, u32[]{:S(2)}) copy-start(f32[768,384]{1,0:T(8,128)S(1)} %get-tuple-element.383) | copy-start | bytes 3538948
  144.3 5.4 copy-start.152
  144.3 5.4 copy-start.154
  144.4 5.3 copy-start.403
  154.4 10.3 copy-start.519
  154.4 10.3 copy-start.521
  164.7 25.1 %copy-start.399 = (f32[768,128]{1,0:T(8,128)}, f32[768,128]{1,0:T(8,128)S(1)}, u32[]{:S(2)}) copy-start(f32[768,128]{1,0:T(8,128)S(1)} %get-tuple-element.726) | copy-start | bytes 1179652
  192.9 157.4 %reduce-scatter.3.cloned.1.call-start = ((), (), s32[]{:S(2)}) async-start(), calls=%async_computation.6 | async-start | bytes 1966080 | tf_op jit(solution)/shard_map/reduce_scatter | solution.py:201
  193.0 57.7 %copy-start.555 = (f32[384]{0:T(512)}, f32[384]{0:T(512)S(1)}, u32[]{:S(2)}) copy-start(f32[384]{0:T(512)S(1)} %get-tuple-element.700) | copy-start | bytes 4612
  193.0 57.7 %copy-start.557 = (f32[384]{0:T(512)}, f32[384]{0:T(512)S(1)}, u32[]{:S(2)}) copy-start(f32[384]{0:T(512)S(1)} %get-tuple-element.701) | copy-start | bytes 4612
  254.6 27.2 %copy-start.18 = (f32[768,384]{1,0:T(8,128)}, f32[768,384]{1,0:T(8,128)S(1)}, u32[]{:S(2)}) copy-start(f32[768,384]{1,0:T(8,128)S(1)} %get-tuple-element.602) | copy-start | bytes 3538948
  254.6 27.2 %copy-start.22 = (f32[768,384]{1,0:T(8,128)}, f32[768,384]{1,0:T(8,128)S(1)}, u32[]{:S(2)}) copy-start(f32[768,384]{1,0:T(8,128)S(1)} %get-tuple-element.601) | copy-start | bytes 3538948
  254.7 5.9 copy-start.126
  254.8 5.8 copy-start.128
  260.5 21.6 %copy-start.4 = (f32[768,384]{1,0:T(8,128)}, f32[768,384]{1,0:T(8,128)S(1)}, u32[]{:S(2)}) copy-start(f32[768,384]{1,0:T(8,128)S(1)} %get-tuple-element.320) | copy-start | bytes 3538948
  260.5 21.6 %copy-start.6 = (f32[768,384]{1,0:T(8,128)}, f32[768,384]{1,0:T(8,128)S(1)}, u32[]{:S(2)}) copy-start(f32[768,384]{1,0:T(8,128)S(1)} %get-tuple-element.321) | copy-start | bytes 3538948
  260.5 22.4 %copy-start.30 = (f32[768,384]{1,0:T(8,128)}, f32[768,384]{1,0:T(8,128)S(1)}, u32[]{:S(2)}) copy-start(f32[768,384]{1,0:T(8,128)S(1)} %get-tuple-element.319) | copy-start | bytes 3538948
  279.4 19.5 %copy-start.156 = (f32[768,384]{1,0:T(8,128)}, f32[768,384]{1,0:T(8,128)S(1)}, u32[]{:S(2)}) copy-start(f32[768,384]{1,0:T(8,128)S(1)} %get-tuple-element.326) | copy-start | bytes 3538948
  279.4 19.5 %copy-start.158 = (f32[768,384]{1,0:T(8,128)}, f32[768,384]{1,0:T(8,128)S(1)}, u32[]{:S(2)}) copy-start(f32[768,384]{1,0:T(8,128)S(1)} %get-tuple-element.327) | copy-start | bytes 3538948
  304.8 10.8 copy-start.527
  304.8 10.8 copy-start.587
  307.4 10.9 copy-start.547
  307.4 10.9 copy-start.548
  321.4 130.2 %all-reduce.326.cloned.1.call-start = ((), (), s32[]{:S(2)}) async-start(), calls=%async_computation.7 | async-start | bytes 9437184 | tf_op jit(solution)/shard_map/psum | solution.py:138
  357.5 322.0 %all-gather.7.cloned.1.call-start = ((), (), s32[]{:S(2)}) async-start(), calls=%async_computation.9 | async-start | bytes 1966080 | tf_op jit(solution)/shard_map/all_gather | solution.py:120
  451.6 9.3 copy-start.251
  468.4 5.1 copy-start.504
  472.0 18.4 %copy-start.349 = (f32[768,384]{1,0:T(8,128)}, f32[768,384]{1,0:T(8,128)S(1)}, u32[]{:S(2)}) copy-start(f32[768,384]{1,0:T(8,128)S(1)} %get-tuple-element.654) | copy-start | bytes 3538948
  659.3 42.1 %all-gather.5.cloned.1.call-start = ((), (), s32[]{:S(2)}) async-start(), calls=%async_computation.8 | async-start | bytes 1966080 | tf_op jit(solution)/shard_map/all_gather | solution.py:119
  659.9 76.4 %reduce-scatter.5.cloned.1.call-start = ((), (), s32[]{:S(2)}) async-start(), calls=%async_computation.10 | async-start | bytes 1966080 | tf_op jit(solution)/shard_map/reduce_scatter | solution.py:201
  679.5 23.5 %copy-start.528 = (bf16[768,128]{1,0:T(8,128)(2,1)S(1)}, bf16[768,128]{1,0:T(8,128)(2,1)}, u32[]{:S(2)}) copy-start(bf16[768,128]{1,0:T(8,128)(2,1)} %param.20) | copy-start | bytes 589828
  681.1 21.9 %copy-start.495 = (f32[768,128]{1,0:T(8,128)S(1)}, f32[768,128]{1,0:T(8,128)}, u32[]{:S(2)}) copy-start(f32[768,128]{1,0:T(8,128)} %get-tuple-element.682) | copy-start | bytes 1179652
  681.1 21.9 %copy-start.520 = (f32[768,128]{1,0:T(8,128)S(1)}, f32[768,128]{1,0:T(8,128)}, u32[]{:S(2)}) copy-start(f32[768,128]{1,0:T(8,128)} %copy-done.519) | copy-start | bytes 1179652
  681.2 21.9 %copy-start.522 = (f32[768,128]{1,0:T(8,128)S(1)}, f32[768,128]{1,0:T(8,128)}, u32[]{:S(2)}) copy-start(f32[768,128]{1,0:T(8,128)} %copy-done.521) | copy-start | bytes 1179652
  681.2 21.9 %copy-start.523 = (f32[768,128]{1,0:T(8,128)S(1)}, f32[768,128]{1,0:T(8,128)}, u32[]{:S(2)}) copy-start(f32[768,128]{1,0:T(8,128)} %get-tuple-element.727) | copy-start | bytes 1179652
  704.9 31.4 %copy-start.496 = (f32[768,128]{1,0:T(8,128)}, f32[768,128]{1,0:T(8,128)S(1)}, u32[]{:S(2)}) copy-start(f32[768,128]{1,0:T(8,128)S(1)} %get-tuple-element.286) | copy-start | bytes 1179652
  708.0 128.3 %all-reduce.328.cloned.1.call-start = ((), (), s32[]{:S(2)}) async-start(), calls=%async_computation.11 | async-start | bytes 9437184 | tf_op jit(solution)/shard_map/psum | solution.py:138
  742.2 94.2 %copy-start.450 = (f32[256,384]{1,0:T(8,128)S(1)}, f32[256,384]{1,0:T(8,128)}, u32[]{:S(2)}) copy-start(f32[256,384]{1,0:T(8,128)} %copy-done.449) | copy-start | bytes 1179652
  742.2 94.2 %copy-start.452 = (f32[256,384]{1,0:T(8,128)S(1)}, f32[256,384]{1,0:T(8,128)}, u32[]{:S(2)}) copy-start(f32[256,384]{1,0:T(8,128)} %copy-done.451) | copy-start | bytes 1179652
  742.2 348.3 %all-gather.11.cloned.1.call-start = ((), (), s32[]{:S(2)}) async-start(), calls=%async_computation.13 | async-start | bytes 1966080 | tf_op jit(solution)/shard_map/all_gather | solution.py:120
  836.4 8.8 copy-start.247
  1036.3 55.8 %all-gather.9.cloned.1.call-start = ((), (), s32[]{:S(2)}) async-start(), calls=%async_computation.12 | async-start | bytes 1966080 | tf_op jit(solution)/shard_map/all_gather | solution.py:119
  1036.9 169.1 %all-reduce.330.cloned.1.call-start = ((), (), s32[]{:S(2)}) async-start(), calls=%async_computation.14 | async-start | bytes 5767168 | tf_op jit(solution)/shard_map/psum | solution.py:223
  1049.0 38.4 %copy-start.561 = (f32[2,3,384]{2,0,1:T(2,128)S(1)}, f32[2,3,384]{2,0,1:T(2,128)}, u32[]{:S(2)}) copy-start(f32[2,3,384]{2,0,1:T(2,128)} %param.37) | copy-start | bytes 27652
  1049.0 38.4 %copy-start.562 = (f32[2,3,384]{2,0,1:T(2,128)S(1)}, f32[2,3,384]{2,0,1:T(2,128)}, u32[]{:S(2)}) copy-start(f32[2,3,384]{2,0,1:T(2,128)} %param.32) | copy-start | bytes 27652
  1049.0 40.8 %copy-start.560 = (f32[2,4,128]{2,1,0:T(4,128)S(1)}, f32[2,4,128]{2,1,0:T(4,128)}, u32[]{:S(2)}) copy-start(f32[2,4,128]{2,1,0:T(4,128)} %param.26) | copy-start | bytes 12292
  1049.0 40.8 %copy-start.575 = (f32[2,4,128]{2,1,0:T(4,128)S(1)}, f32[2,4,128]{2,1,0:T(4,128)}, u32[]{:S(2)}) copy-start(f32[2,4,128]{2,1,0:T(4,128)} %param.36) | copy-start | bytes 12292
  1049.1 40.8 %copy-start.576 = (f32[2,4,128]{2,1,0:T(4,128)S(1)}, f32[2,4,128]{2,1,0:T(4,128)}, u32[]{:S(2)}) copy-start(f32[2,4,128]{2,1,0:T(4,128)} %param.31) | copy-start | bytes 12292
  1092.1 114.0 %copy-start.513 = (f32[2,512,128]{2,1,0:T(8,128)S(1)}, f32[2,512,128]{2,1,0:T(8,128)}, u32[]{:S(2)}) copy-start(f32[2,512,128]{2,1,0:T(8,128)} %param.25) | copy-start | bytes 1572868
  1092.1 114.0 %copy-start.545 = (f32[2,512,128]{2,1,0:T(8,128)S(1)}, f32[2,512,128]{2,1,0:T(8,128)}, u32[]{:S(2)}) copy-start(f32[2,512,128]{2,1,0:T(8,128)} %param.35) | copy-start | bytes 1572868
  1092.1 113.9 %copy-start.546 = (f32[2,512,128]{2,1,0:T(8,128)S(1)}, f32[2,512,128]{2,1,0:T(8,128)}, u32[]{:S(2)}) copy-start(f32[2,512,128]{2,1,0:T(8,128)} %param.30) | copy-start | bytes 1572868
  (538 other events, 1074.6 us)
Sparse Core Ops, SparseCore 0:
  39.4 56.7 all-reduce.321
  193.0 55.6 all-reduce.323
  321.6 28.6 reduce-scatter.2
  357.6 94.0 all-reduce.325
  659.5 19.9 all-gather.6
  681.6 19.8 all-gather.4
  708.1 28.1 reduce-scatter.4
  742.3 94.0 all-reduce.327
  1036.4 19.9 all-gather.10
  1058.5 19.8 all-gather.8
  1082.9 123.1 all-reduce.329
